TPU v7x, 32 devices: a whole 2x2x4 slice. The times are simulated.
32 devices in a mesh: grp: 2 (over y), feat: 4 (over z), samp: 4 (over x, core).
Axes of the slice: x: 2, y: 2, z: 4, core: 2. Of those that a mesh axis runs over, the one named last changes fastest.
Arguments:
- embeddings: bfloat16 [8192, 1024], P(('grp', 'samp')), parts along dimension 0, may hold values from -6 to 6
- sign_bits: int32 [4096], P('feat'), may hold values 0 or 1
- perms: int32 [4, 1024], P('feat'), may hold values from 0 to 1023, each once within a row
- gauss: float32 [4096], P('feat'), may hold values from -4 to 4
- scale: float32 [4096], P('feat'), may hold values from 0.5 to 2
- phase: float32 [4096], P('feat'), may hold values from -3.140625 to 3.140625
- basis: float32 [128, 4096], P('grp', 'feat'), parts along dimension 0, may hold values from -40 to 40
Outputs:
- basis_out: float32 [128, 4096], P('grp', 'feat'), parts along dimension 0
- projections: float32 [128, 4096], P('grp', 'samp'), parts along dimension 0
There are 2 independent parts, one for each index of `grp`. A program takes and returns all parts, laid end to end along the dimension named above; an argument that names none is the same for every part. Nothing has to cross between parts.
Inputs may be any that keep to these rules, and one draw needn't show every extreme that they name: Each row of perms names every number of 0 to 1023 once.
All inputs are finite; a program needn't handle non-finite values. No bound on the sum of `sign_bits` on one device may be relied on, other than what follows from the above.
Results may differ from a plain program's by a relative error of at most 0.0057.
Values sent between devices are 32-bit elements; how exact they have to be, the bound alone decides.
A program may use at most 64 MiB of HBM per device.

v0:
```python
import math
import jax
import jax.numpy as jnp
from jax import lax
from jax.sharding import PartitionSpec as P


def sylvester(width):
    indices = lax.iota(jnp.int32, width)
    parity = jnp.zeros((width, width), jnp.int32)
    for position in range(width.bit_length() - 1):
        row_bits = jnp.right_shift(indices[:, None], position) & 1
        col_bits = jnp.right_shift(indices[None, :], position) & 1
        parity = parity + row_bits * col_bits
    return jnp.where(parity % 2 == 0, 1.0, -1.0).astype(jnp.bfloat16)


def cholesky_step(grown, total):
    local_gram = jnp.dot(grown, grown.T, precision=lax.Precision.HIGHEST)
    gram = lax.psum(local_gram, "feat")
    lower = jnp.linalg.cholesky(gram / total)
    return jax.scipy.linalg.solve_triangular(lower, grown, lower=True)


def local(embeddings, sign_bits, perms, gauss, scale, phase, basis):
    width = embeddings.shape[1]
    rows = embeddings.shape[0]
    table = sylvester(width)
    features_total = width * lax.axis_size("feat")
    span_total = rows * lax.axis_size("samp")
    signs = (2 * sign_bits - 1).astype(jnp.bfloat16)
    first = jnp.dot(embeddings * signs, table, preferred_element_type=jnp.float32).astype(
        jnp.bfloat16
    )
    reorder = (lax.iota(jnp.int32, width)[:, None] == perms[0][None, :]).astype(jnp.bfloat16)
    picked = jnp.dot(first, reorder, preferred_element_type=jnp.float32)
    mixed = (picked * gauss).astype(jnp.bfloat16)
    freq = jnp.dot(mixed, table, preferred_element_type=jnp.float32) * scale / width + phase
    features = (math.sqrt(2.0) * jnp.cos(freq)).astype(jnp.bfloat16)
    basis_low = basis.astype(jnp.bfloat16)
    partial_scores = lax.dot_general(
        basis_low, features, (((1,), (1,)), ((), ())), preferred_element_type=jnp.float32
    )
    summed = lax.psum(partial_scores, "feat")
    projections = summed / math.sqrt(features_total)
    proj_low = projections.astype(jnp.bfloat16)
    update_part = jnp.dot(proj_low, features, preferred_element_type=jnp.float32)
    update = lax.psum(update_part, "samp")
    grown = basis + update / math.sqrt(span_total)
    basis_out = cholesky_step(grown, features_total)
    return (basis_out, projections)


def solution(mesh):
    placed = (
        P(("grp", "samp"), None),
        P("feat"),
        P("feat", None),
        P("feat"),
        P("feat"),
        P("feat"),
        P("grp", "feat"),
    )
    return jax.shard_map(
        local,
        mesh=mesh,
        in_specs=placed,
        out_specs=(P("grp", "feat"), P("grp", "samp")),
        check_vma=False,
    )
```

profile of v0, /device:TPU:0, one launch (start us, length us, event | category | flops | bytes accessed | tf_op | source)
XLA Modules:
  0.0 159.9 jit_solution(12361996061334306493)
XLA Ops:
  7.2 0.0 all-reduce.3.cloned.1.call-start
  7.3 0.7 add_convert_fusion
  8.0 1.5 iota_compare_fusion.7
  9.5 0.0 copy-start.2
  9.5 0.0 copy-start.3
  9.5 0.0 copy-start.4
  9.5 12.2 %fusion.2 = f32[1024,1024]{1,0:T(8,128)} fusion(bf16[1024,1024]{1,0:T(8,128)(2,1)} %param.7, bf16[1024]{0:T(1024)(128)(2,1)S(1)} %add_convert_fusion, s32[1024]{0:T(1024)S(1)} %get-tuple-element.2, s32[1024]{0:T(1024)S(1)} %get-tuple-element.3, s32[1024]{0:T(1024)S(1)} %get-tuple-element.4, s32[1024]{0:T(1024)S(1)} %get-tuple-element.5, ...), kind=kOutput, calls=%fused_computation.9 | convolution fusion | flops 4331667456 | bytes 7383040 | tf_op jit(solution)/shard_map/dot_general | solution.py:36
  21.7 0.0 copy-done.2
  21.7 0.0 copy-done.3
  21.7 0.0 copy-done.4
  21.7 0.0 copy-start
  21.7 22.2 %multiply_convert_fusion = bf16[1024,1024]{1,0:T(8,128)(2,1)S(1)} fusion(f32[1024,1024]{1,0:T(8,128)} %fusion.2, f32[1024]{0:T(1024)S(1)} %copy-done.2, f32[1024]{0:T(1024)S(1)} %copy-done.3, f32[1024]{0:T(1024)S(1)} %copy-done.4, s32[1024]{0:T(1024)S(1)} %get-tuple-element.2, s32[1024]{0:T(1024)S(1)} %get-tuple-element.3, s32[1024]{0:T(1024)S(1)} %get-tuple-element.4, ...), kind=kOutput, calls=%fused_computation.5 | convolution fusion | flops 2189426688 | bytes 6344704 | tf_op jit(solution)/shard_map/dot_general | solution.py:38
  44.0 0.0 copy-done
  44.0 1.5 convolution_bitcast_fusion
  45.4 0.0 all-reduce.3.cloned.1.call-update
  45.5 0.0 all-reduce.5.cloned.1.call-start
  45.5 38.1 %all-reduce.3.cloned.1.call-done = f32[64,1024]{1,0:T(8,128)} async-done(((f32[64,1024]{1,0:T(8,128)}), f32[64,1024]{1,0:T(8,128)}) %all-reduce.3.cloned.1.call-update) | async-done | bytes 262160 | tf_op jit(solution)/shard_map/psum | solution.py:44
  83.6 1.0 broadcast_multiply_fusion
  84.6 0.0 copy-start.1
  84.6 1.2 fusion.14
  85.8 0.0 all-reduce.5.cloned.1.call-update
  85.8 32.5 %all-reduce.5.cloned.1.call-done = f32[64,1024]{1,0:T(8,128)} async-done(((f32[64,1024]{1,0:T(8,128)}), f32[64,1024]{1,0:T(8,128)}) %all-reduce.5.cloned.1.call-update) | async-done | bytes 262160 | tf_op jit(solution)/shard_map/psum | solution.py:48
  118.4 1.4 fusion.18
  119.8 19.0 %psum.23 = f32[64,64]{0,1:T(8,128)S(1)} all-reduce(f32[64,64]{0,1:T(8,128)S(1)} %fusion.18), channel_id=1, replica_groups=mesh['grp'=2,'feat'=4,'samp'=4] {'feat'}, use_global_device_ids=true, to_apply=%region_2.3 | all-reduce | flops 4096 | bytes 32768 | tf_op jit(solution)/shard_map/psum | solution.py:20
  138.8 0.1 copy.10
  138.9 5.8 %cholesky.16 = f32[64,64]{1,0:T(8,128)S(1)} custom-call(f32[64,64]{1,0:T(8,128)S(1)} %fusion.21), custom_call_target="Cholesky" | custom-call | tf_op jit(solution)/shard_map/jit(cholesky)/cholesky | solution.py:21
  144.7 0.6 compare_reduce_fusion
  145.4 0.7 fusion.19
  146.1 4.9 %custom-call.7 = f32[1,64,64]{1,2,0:T(8,128)S(1)} custom-call(f32[1,64,64]{2,1,0:T(8,128)S(1)} %fusion.19), custom_call_target="InvertDiagBlocksLowerTriangular" | custom-call | tf_op jit(solution)/shard_map/jit(_solve_triangular)/triangular_solve | solution.py:22
  150.9 2.1 %fusion.17 = f32[64,1024]{1,0:T(8,128)} fusion(f32[64,1024]{1,0:T(8,128)S(1)} %copy-done, f32[64,1024]{1,0:T(8,128)} %all-reduce.5.cloned.1.call-done, f32[1,64,64]{1,2,0:T(8,128)S(1)} %custom-call.7), kind=kOutput, calls=%fused_computation.22 | convolution fusion | flops 50462720 | bytes 802816 | tf_op jit(solution)/shard_map/jit(_solve_triangular)/triangular_solve | solution.py:22
  153.0 0.0 copy-done.1
  (8 shorter events, 0.1 us)
Async XLA Ops:
  7.2 76.5 %all-reduce.3.cloned.1.call-start = ((), (), s32[]{:S(2)}) async-start(), calls=%async_computation | async-start | bytes 524288 | tf_op jit(solution)/shard_map/psum | solution.py:44
  9.5 12.3 %copy-start.2 = (f32[1024]{0:T(1024)S(1)}, f32[1024]{0:T(1024)}, u32[]{:S(2)}) copy-start(f32[1024]{0:T(1024)} %param.12) | copy-start | bytes 12292
  9.5 12.3 %copy-start.3 = (f32[1024]{0:T(1024)S(1)}, f32[1024]{0:T(1024)}, u32[]{:S(2)}) copy-start(f32[1024]{0:T(1024)} %param.11) | copy-start | bytes 12292
  9.5 12.3 %copy-start.4 = (f32[1024]{0:T(1024)S(1)}, f32[1024]{0:T(1024)}, u32[]{:S(2)}) copy-start(f32[1024]{0:T(1024)} %param.10) | copy-start | bytes 12292
  21.7 22.2 %copy-start = (f32[64,1024]{1,0:T(8,128)S(1)}, f32[64,1024]{1,0:T(8,128)}, u32[]{:S(2)}) copy-start(f32[64,1024]{1,0:T(8,128)} %param.13) | copy-start | bytes 786436
  45.5 72.9 %all-reduce.5.cloned.1.call-start = ((), (), s32[]{:S(2)}) async-start(), calls=%async_computation.1 | async-start | bytes 524288 | tf_op jit(solution)/shard_map/psum | solution.py:48
  84.6 68.4 %copy-start.1 = (f32[64,1024]{1,0:T(8,128)}, f32[64,1024]{1,0:T(8,128)S(1)}, u32[]{:S(2)}) copy-start(f32[64,1024]{1,0:T(8,128)S(1)} %broadcast_multiply_fusion) | copy-start | bytes 786436
Sparse Core Ops, SparseCore 0:
  45.6 37.9 all-reduce.2
  86.6 31.6 all-reduce.4
where the time goes:
time: 160 us
  waiting for transfers between devices  70.7 us (44%)
  matrix products  40.6 us (25%)
  blocking collectives  19 us (12%)
  other arithmetic  15.3 us (10%)
  between operations  14.2 us (9%)
    psum x1, waiting for transfers between devices, local(): summed = lax.psum(partial_scores, 'feat')  38.1 us
    psum x1, waiting for transfers between devices, local(): update = lax.psum(update_part, 'samp')  32.5 us
    dot_general x1, matrix products, local(): jnp.dot(mixed, table, preferred_element_type=jnp.float32) * scale / width  22.2 us
    psum x1, blocking collectives, cholesky_step(): gram = lax.psum(local_gram, 'feat')  19 us
    dot_general x1, matrix products, local(): picked = jnp.dot(first, reorder, preferred_element_type=jnp.float32)  12.2 us
    another operation x3, other arithmetic, cholesky_step(): lower = jnp.linalg.cholesky(gram / total)  6.52 us
    another operation x2, other arithmetic, cholesky_step(): return jax.scipy.linalg.solve_triangular(lower, grown, lower=True)  5.55 us
  transfers between devices with their start and end apart: 2, of which 2 were waited for; matrix products, arithmetic and copies ran while one was open for 0% of the time, Pallas kernels for 0%

commit v1 on v0

--- a/solution.py
+++ b/solution.py
@@ -45,7 +45,8 @@
     projections = summed / math.sqrt(features_total)
     proj_low = projections.astype(jnp.bfloat16)
     update_part = jnp.dot(proj_low, features, preferred_element_type=jnp.float32)
-    update = lax.psum(update_part, "samp")
+    parts = lax.all_gather(update_part, "samp", axis=0, tiled=False)
+    update = parts.sum(axis=0)
     grown = basis + update / math.sqrt(span_total)
     basis_out = cholesky_step(grown, features_total)
     return (basis_out, projections)

time: 160 us -> 144 us (0.900)
  waiting for transfers between devices: 70.7 us -> 54.8 us
  matrix products: 40.6 us -> 38.6 us
    psum x1 -> x0, waiting for transfers between devices: 32.5 us -> none  [local(): update = lax.psum(update_part, 'samp')]
    all_gather x0 -> x1, waiting for transfers between devices: none -> 16.6 us  [local(): parts = lax.all_gather(update_part, 'samp', axis=0, tiled=False)]
where the time goes in v1:
time: 144 us; the launch traced here: 143 us
  waiting for transfers between devices  54.8 us (38%)
  matrix products  38.6 us (27%)
  blocking collectives  19 us (13%)
  other arithmetic  16.6 us (12%)
  between operations  14.2 us (10%)
    psum x1, waiting for transfers between devices, local(): summed = lax.psum(partial_scores, 'feat')  38.1 us
    dot_general x1, matrix products, local(): jnp.dot(mixed, table, preferred_element_type=jnp.float32) * scale / width  22.2 us
    psum x1, blocking collectives, cholesky_step(): gram = lax.psum(local_gram, 'feat')  19 us
    all_gather x1, waiting for transfers between devices, local(): parts = lax.all_gather(update_part, 'samp', axis=0, tiled=False)  16.6 us
    dot_general x1, matrix products, local(): picked = jnp.dot(first, reorder, preferred_element_type=jnp.float32)  12.2 us
    another operation x3, other arithmetic, cholesky_step(): lower = jnp.linalg.cholesky(gram / total)  6.52 us
    another operation x2, other arithmetic, cholesky_step(): return jax.scipy.linalg.solve_triangular(lower, grown, lower=True)  5.55 us
  transfers between devices with their start and end apart: 2, of which 2 were waited for; matrix products, arithmetic and copies ran while one was open for 0% of the time, Pallas kernels for 0%

profile of v1, /device:TPU:0, one launch (start us, length us, event | category | flops | bytes accessed | tf_op | source)
XLA Modules:
  0.0 143.3 jit_solution(6783431924705769275)
XLA Ops:
  7.2 0.0 all-reduce.2.cloned.1.call-start
  7.3 0.7 add_convert_fusion
  8.0 1.5 %iota_compare_fusion.7 = pred[1024,1024]{1,0:T(32,128)(4,1)S(1)} fusion(s32[1024]{0:T(1024)} %bitcast.17), kind=kLoop, calls=%fused_computation.7.clone.clone.2 | loop fusion | flops 1048576 | bytes 1052672 | tf_op jit(solution)/shard_map/dot_general | solution.py:36
  9.5 0.0 copy-start.2
  9.5 0.0 copy-start.3
  9.5 0.0 copy-start.4
  9.5 12.2 %fusion.2 = f32[1024,1024]{1,0:T(8,128)} fusion(bf16[1024,1024]{1,0:T(8,128)(2,1)} %param.7, bf16[1024]{0:T(1024)(128)(2,1)S(1)} %add_convert_fusion, s32[1024]{0:T(1024)S(1)} %get-tuple-element.2, s32[1024]{0:T(1024)S(1)} %get-tuple-element.3, s32[1024]{0:T(1024)S(1)} %get-tuple-element.4, s32[1024]{0:T(1024)S(1)} %get-tuple-element.5, ...), kind=kOutput, calls=%fused_computation.9 | convolution fusion | flops 4331667456 | bytes 7383040 | tf_op jit(solution)/shard_map/dot_general | solution.py:36
  21.7 0.0 copy-done.2
  21.7 0.0 copy-done.3
  21.7 0.0 copy-done.4
  21.7 0.0 copy-start
  21.7 22.2 %multiply_convert_fusion = bf16[1024,1024]{1,0:T(8,128)(2,1)S(1)} fusion(f32[1024,1024]{1,0:T(8,128)} %fusion.2, f32[1024]{0:T(1024)S(1)} %copy-done.2, f32[1024]{0:T(1024)S(1)} %copy-done.3, f32[1024]{0:T(1024)S(1)} %copy-done.4, s32[1024]{0:T(1024)S(1)} %get-tuple-element.2, s32[1024]{0:T(1024)S(1)} %get-tuple-element.3, s32[1024]{0:T(1024)S(1)} %get-tuple-element.4, ...), kind=kOutput, calls=%fused_computation.5 | convolution fusion | flops 2189426688 | bytes 6344704 | tf_op jit(solution)/shard_map/dot_general | solution.py:38
  44.0 0.0 copy-done
  44.0 1.5 %convolution_bitcast_fusion = f32[64,1024]{1,0:T(8,128)} fusion(bf16[1024,1024]{1,0:T(8,128)(2,1)S(1)} %multiply_convert_fusion, f32[64,1024]{1,0:T(8,128)S(1)} %copy-done), kind=kOutput, calls=%fused_computation.15 | convolution fusion | flops 134283264 | bytes 2621440 | tf_op jit(solution)/shard_map/dot_general | solution.py:41
  45.4 0.0 all-reduce.2.cloned.1.call-update
  45.5 0.0 all-gather.3.cloned.1.call-start
  45.5 38.1 %all-reduce.2.cloned.1.call-done = f32[64,1024]{1,0:T(8,128)} async-done(((f32[64,1024]{1,0:T(8,128)}), f32[64,1024]{1,0:T(8,128)}) %all-reduce.2.cloned.1.call-update) | async-done | bytes 262160 | tf_op jit(solution)/shard_map/psum | solution.py:44
  83.6 1.0 broadcast_multiply_fusion
  84.6 0.0 copy-start.1
  84.6 1.2 fusion.14
  85.8 0.0 all-gather.3.cloned.1.call-update
  85.8 16.6 %all-gather.3.cloned.1.call-done = f32[256,1024]{1,0:T(8,128)} async-done(((f32[64,1024]{1,0:T(8,128)}), f32[256,1024]{1,0:T(8,128)}) %all-gather.3.cloned.1.call-update) | async-done | bytes 1048592 | tf_op jit(solution)/shard_map/all_gather | solution.py:48
  102.4 1.3 reduce_sum.9
  103.7 0.4 fusion.18
  104.1 19.0 %psum.15 = f32[64,64]{0,1:T(8,128)S(1)} all-reduce(f32[64,64]{0,1:T(8,128)S(1)} %fusion.18), channel_id=1, replica_groups=mesh['grp'=2,'feat'=4,'samp'=4] {'feat'}, use_global_device_ids=true, to_apply=%region_2.3 | all-reduce | flops 4096 | bytes 32768 | tf_op jit(solution)/shard_map/psum | solution.py:20
  123.1 0.1 copy.10
  123.2 5.8 %cholesky.16 = f32[64,64]{1,0:T(8,128)S(1)} custom-call(f32[64,64]{1,0:T(8,128)S(1)} %fusion.21), custom_call_target="Cholesky" | custom-call | tf_op jit(solution)/shard_map/jit(cholesky)/cholesky | solution.py:21
  129.1 0.6 compare_reduce_fusion
  129.7 0.7 fusion.19
  130.4 4.9 %custom-call.7 = f32[1,64,64]{1,2,0:T(8,128)S(1)} custom-call(f32[1,64,64]{2,1,0:T(8,128)S(1)} %fusion.19), custom_call_target="InvertDiagBlocksLowerTriangular" | custom-call | tf_op jit(solution)/shard_map/jit(_solve_triangular)/triangular_solve | solution.py:22
  135.3 1.1 fusion.17
  136.4 0.0 copy-done.1
  (8 shorter events, 0.1 us)
Async XLA Ops:
  7.2 76.5 %all-reduce.2.cloned.1.call-start = ((), (), s32[]{:S(2)}) async-start(), calls=%async_computation | async-start | bytes 524288 | tf_op jit(solution)/shard_map/psum | solution.py:44
  9.5 12.3 %copy-start.2 = (f32[1024]{0:T(1024)S(1)}, f32[1024]{0:T(1024)}, u32[]{:S(2)}) copy-start(f32[1024]{0:T(1024)} %param.12) | copy-start | bytes 12292
  9.5 12.3 %copy-start.3 = (f32[1024]{0:T(1024)S(1)}, f32[1024]{0:T(1024)}, u32[]{:S(2)}) copy-start(f32[1024]{0:T(1024)} %param.11) | copy-start | bytes 12292
  9.5 12.3 %copy-start.4 = (f32[1024]{0:T(1024)S(1)}, f32[1024]{0:T(1024)}, u32[]{:S(2)}) copy-start(f32[1024]{0:T(1024)} %param.10) | copy-start | bytes 12292
  21.7 22.2 %copy-start = (f32[64,1024]{1,0:T(8,128)S(1)}, f32[64,1024]{1,0:T(8,128)}, u32[]{:S(2)}) copy-start(f32[64,1024]{1,0:T(8,128)} %param.13) | copy-start | bytes 786436
  45.5 57.0 %all-gather.3.cloned.1.call-start = ((), (), s32[]{:S(2)}) async-start(), calls=%async_computation.1 | async-start | bytes 1310720 | tf_op jit(solution)/shard_map/all_gather | solution.py:48
  84.6 51.8 %copy-start.1 = (f32[64,1024]{1,0:T(8,128)}, f32[64,1024]{1,0:T(8,128)S(1)}, u32[]{:S(2)}) copy-start(f32[64,1024]{1,0:T(8,128)S(1)} %broadcast_multiply_fusion) | copy-start | bytes 786436
Sparse Core Ops, SparseCore 0:
  45.6 37.9 all-reduce.1
  85.9 16.4 all-gather.2
